TPU v7x, 32 devices: a whole 2x2x4 slice. The times are simulated.
32 devices in a mesh: pipe: 2 (over core), expert: 16 (over z, y, x).
Axes of the slice: x: 2, y: 2, z: 4, core: 2. Of those that a mesh axis runs over, the one named last changes fastest.
Arguments:
- hidden_a: bfloat16 [2, 1024, 3584], P('pipe', 'expert'), may hold values from -6 to 6
- routes_a: int32 [2, 1024, 8], P('pipe', 'expert'), may hold values from 0 to 15, all different within a row; in each aligned block of 64 rows (0 to 63, 64 to 127, ..., all dimensions but the last counted through in order) at most 48 rows name the same one
- hidden_b: bfloat16 [2, 1024, 3584], P('pipe', 'expert'), may hold values from -6 to 6
- routes_b: int32 [2, 1024, 8], P('pipe', 'expert'), may hold values from 0 to 15, all different within a row; in each aligned block of 64 rows (0 to 63, 64 to 127, ..., all dimensions but the last counted through in order) at most 48 rows name the same one
- grad_out_b: bfloat16 [2, 1024, 3584], P('pipe', 'expert'), may hold values from -0.796875 to 0.796875
- router: bfloat16 [2, 16, 3584], P('pipe'), as said below
- w_up: bfloat16 [2, 16, 3584, 1024], P('pipe', 'expert'), as said below
- w_down: bfloat16 [2, 16, 1024, 3584], P('pipe', 'expert'), as said below
Outputs:
- layer_out_a: bfloat16 [2, 1024, 3584], P('pipe', 'expert')
- grad_in_b: bfloat16 [2, 1024, 3584], P('pipe', 'expert')
- router_grad: float32 [2, 16, 3584], P('pipe', 'expert')
Inputs may be any that keep to these rules, and one draw needn't show every extreme that they name: `routes_a`: each token names 8 different experts. Among the 64 tokens of one device no expert is named by more than 48 tokens, and in every draw some expert is named by exactly 48 tokens of some device. `routes_b`: as for routes_a. router[1 - p] equals router[p] for every p. w_up[1 - p] equals w_up[p] for every p. w_down[1 - p] equals w_down[p] for every p.
All inputs are finite; a program needn't handle non-finite values.
Results may differ from a plain program's by a relative error of at most 0.014.
Values may be sent and summed in bfloat16 or wider, within the bound.
A program may use at most 128 MiB of HBM per device.

v0:
```python
import jax
import jax.numpy as jnp
from jax import lax
from jax.sharding import PartitionSpec as P

ROUTED_SCALE = 2.5
EPSILON = 1e-06


def partner(block, axis, bit):
    count = lax.axis_size(axis)
    route = []
    for low in range(count):
        high = low | 1 << bit
        if high != low and high < count:
            route += [(low, high), (high, low)]
    return lax.ppermute(block, axis, route)


def silu_slope(pre):
    sig = jax.nn.sigmoid(pre)
    return sig * (1.0 + pre * (1.0 - sig))


def slot_tables(routes, expert_count, capacity):
    routes_flat = routes.reshape(-1)
    onehot = (routes_flat[:, None] == jnp.arange(expert_count, dtype=jnp.int32)[None, :]).astype(
        jnp.int32
    )
    slot_rank = jnp.sum((jnp.cumsum(onehot, axis=0) - 1) * onehot, axis=1)
    slot_index = routes_flat * capacity + slot_rank
    owner_tokens = jnp.arange(routes_flat.shape[0], dtype=jnp.int32) // routes.shape[1]
    owners = jnp.zeros((expert_count * capacity,), jnp.int32).at[slot_index].set(owner_tokens)
    return (slot_index, owners)


def prepare(hidden, routes, router_segment, capacity):
    expert_count = router_segment.shape[0]
    hidden32 = hidden.astype(jnp.float32)
    rinv = lax.rsqrt(jnp.mean(hidden32 * hidden32, axis=-1, keepdims=True) + EPSILON)
    normed = (hidden32 * rinv).astype(jnp.bfloat16)
    logits = jnp.einsum("td,ed->te", normed, router_segment, preferred_element_type=jnp.float32)
    picked = jnp.take_along_axis(logits, routes, axis=1)
    affinity = jax.nn.sigmoid(picked)
    aff_total = jnp.sum(affinity, axis=1, keepdims=True)
    weight = affinity / aff_total
    slot_index, owners = slot_tables(routes, expert_count, capacity)
    return (hidden32, rinv, normed, affinity, aff_total, weight, slot_index, owners)


def on_device(hidden_a, routes_a, hidden_b, routes_b, grad_out_b, router, w_up, w_down):
    n_expert = lax.axis_size("expert")
    tok_count = hidden_a.shape[1]
    model_dim = hidden_a.shape[2]
    top_count = routes_a.shape[2]
    router_segment = router[0]
    expert_count = router_segment.shape[0]
    local_count = w_up.shape[1]
    capacity = min(tok_count, 3 * tok_count * top_count // (2 * expert_count))
    up_local = w_up[0]
    down_local = w_down[0]
    slab_shape = (n_expert, local_count, capacity, model_dim)
    hidden32_a, rinv_a, normed_a, affinity_a, total_a, weight_a, slot_a, owners_a = prepare(
        hidden_a[0], routes_a[0], router_segment, capacity
    )
    hidden32_b, rinv_b, normed_b, affinity_b, total_b, weight_b, slot_b, owners_b = prepare(
        hidden_b[0], routes_b[0], router_segment, capacity
    )
    grad_out = grad_out_b[0]
    send_a = jnp.take(normed_a, owners_a, axis=0).reshape(slab_shape)
    send_b = jnp.take(normed_b, owners_b, axis=0).reshape(slab_shape)
    send_grad = jnp.take(grad_out, owners_b, axis=0).reshape(slab_shape)
    pre = jnp.einsum(
        "secd,edf->secf",
        lax.all_to_all(send_a, "expert", split_axis=0, concat_axis=0, tiled=True),
        up_local,
        preferred_element_type=jnp.float32,
    )
    active = jax.nn.silu(pre).astype(jnp.bfloat16)
    return_a = lax.all_to_all(
        jnp.einsum("secf,efd->secd", active, down_local, preferred_element_type=jnp.float32).astype(
            jnp.bfloat16
        ),
        "expert",
        split_axis=0,
        concat_axis=0,
        tiled=True,
    )
    pre = jnp.einsum(
        "secd,edf->secf",
        lax.all_to_all(send_b, "expert", split_axis=0, concat_axis=0, tiled=True),
        up_local,
        preferred_element_type=jnp.float32,
    )
    active = jax.nn.silu(pre).astype(jnp.bfloat16)
    back = jnp.einsum(
        "secd,efd->secf",
        lax.all_to_all(send_grad, "expert", split_axis=0, concat_axis=0, tiled=True),
        down_local,
        preferred_element_type=jnp.float32,
    )
    score = jnp.sum(back * active.astype(jnp.float32), axis=-1).astype(jnp.bfloat16)
    inner = (back * silu_slope(pre)).astype(jnp.bfloat16)
    lifted = jnp.einsum(
        "secf,edf->secd", inner, up_local, preferred_element_type=jnp.float32
    ).astype(jnp.bfloat16)
    lifted, score = (lifted, score)
    lifted_b = lax.all_to_all(lifted, "expert", split_axis=0, concat_axis=0, tiled=True)
    score_b = lax.all_to_all(score, "expert", split_axis=0, concat_axis=0, tiled=True)
    expert_out = return_a.reshape(-1, model_dim)[slot_a].reshape(tok_count, top_count, model_dim)
    mixed = hidden32_a + ROUTED_SCALE * jnp.sum(
        weight_a[:, :, None] * expert_out.astype(jnp.float32), axis=1
    )
    layer_out = mixed.astype(jnp.bfloat16)
    lifted_pairs = lifted_b.reshape(-1, model_dim)[slot_b].reshape(tok_count, top_count, model_dim)
    score_pairs = score_b.reshape(-1)[slot_b].reshape(tok_count, top_count)
    gate_grad = ROUTED_SCALE * score_pairs.astype(jnp.float32)
    logit_grad = (
        affinity_b
        * (1.0 - affinity_b)
        * (gate_grad - jnp.sum(gate_grad * weight_b, axis=1, keepdims=True))
        / total_b
    )
    chosen = (
        routes_b[0][:, :, None] == jnp.arange(expert_count, dtype=jnp.int32)[None, None, :]
    ).astype(jnp.float32)
    dense = jnp.sum(chosen * logit_grad[:, :, None], axis=1)
    normed_grad = ROUTED_SCALE * jnp.sum(
        weight_b[:, :, None] * lifted_pairs.astype(jnp.float32), axis=1
    )
    normed_grad = normed_grad + jnp.dot(
        dense, router_segment.astype(jnp.float32), precision=lax.Precision.HIGHEST
    )
    mean_term = jnp.mean(normed_grad * hidden32_b, axis=-1, keepdims=True)
    grad_in = (
        grad_out.astype(jnp.float32) + rinv_b * normed_grad - hidden32_b * rinv_b**3 * mean_term
    )
    normed_b32 = normed_b.astype(jnp.float32)
    pipe_bits = lax.axis_size("pipe").bit_length() - 1
    own_term = jnp.dot(dense.T, normed_b32, precision=lax.Precision.HIGHEST)
    mirrored = own_term
    for bit in range(pipe_bits):
        mirrored = partner(mirrored.astype(jnp.bfloat16), "pipe", bit).astype(mirrored.dtype)
    router_grad = lax.psum_scatter(
        (own_term + mirrored).astype(jnp.bfloat16), "expert", scatter_dimension=0, tiled=True
    ).astype(jnp.float32)
    return (layer_out[None], grad_in.astype(jnp.bfloat16)[None], router_grad[None])


def solution(mesh):
    placed = (
        P("pipe", "expert", None),
        P("pipe", "expert", None),
        P("pipe", "expert", None),
        P("pipe", "expert", None),
        P("pipe", "expert", None),
        P("pipe", None, None),
        P("pipe", "expert", None, None),
        P("pipe", "expert", None, None),
    )
    return jax.shard_map(
        on_device,
        mesh=mesh,
        in_specs=placed,
        out_specs=(P("pipe", "expert", None), P("pipe", "expert", None), P("pipe", "expert", None)),
        check_vma=False,
    )
```

profile of v0, /device:TPU:0, one launch (start us, length us, event | category | flops | bytes accessed | tf_op | source)
XLA Modules:
  0.0 793.3 jit_solution(14581432311804363749)
XLA Ops:
  11.2 2.4 scatter_custom_fusion.1
  13.6 1.2 fusion.52
  15.5 1.2 fusion.53
  16.6 5.4 gather_fusion.7
  22.1 5.5 gather_fusion.6
  27.5 7.7 broadcast_select_fusion
  35.2 130.6 %all_to_all.30 = bf16[16,1,48,3584]{3,2,1,0:T(8,128)(2,1)} all-to-all(bf16[16,1,48,3584]{3,2,1,0:T(8,128)(2,1)S(1)} %bitcast.272), channel_id=1, replica_groups=mesh['pipe'=2,'expert'=16] {'expert'}, dimensions={0} | all-to-all | bytes 11010048 | tf_op jit(solution)/shard_map/all_to_all | solution.py:91
  165.8 4.8 all-to-all-start.2
  172.6 2.4 scatter_custom_fusion
  175.4 5.4 gather_fusion.4
  180.9 5.5 broadcast_select_fusion.2
  186.3 85.0 %all-to-all-done.2 = bf16[16,1,48,3584]{3,2,1,0:T(8,128)(2,1)} async-done(((bf16[16,1,48,3584]{3,2,1,0:T(8,128)(2,1)}), bf16[16,1,48,3584]{3,2,1,0:T(8,128)(2,1)}, u32[]{:S(2)}, u32[]{:S(2)}) %all-to-all-start.2) | async-done | bytes 5505056 | tf_op jit(solution)/shard_map/all_to_all | solution.py:98
  271.3 25.3 %all-to-all-start = ((bf16[16,1,48,3584]{3,2,1,0:T(8,128)(2,1)}), bf16[16,1,48,3584]{3,2,1,0:T(8,128)(2,1)}, u32[]{:S(2)}, u32[]{:S(2)}) async-start(bf16[16,1,48,3584]{3,2,1,0:T(8,128)(2,1)} %bitcast.271), calls=%async_computation | async-start | bytes 11010048 | tf_op jit(solution)/shard_map/all_to_all | solution.py:75
  296.6 9.7 %fusion.4 = f32[16,48,1024]{2,1,0:T(8,128)S(1)} fusion(bf16[1,1,3584,1024]{3,2,1,0:T(8,128)(2,1)} %param.18, bf16[16,1,48,3584]{3,2,1,0:T(8,128)(2,1)} %all_to_all.30), kind=kOutput, calls=%fused_computation.16 | convolution fusion | flops 5637144576 | bytes 15990784 | tf_op jit(solution)/shard_map/secd,edf->secf/dot_general | solution.py:89
  306.3 12.5 %fusion.28 = (bf16[16,48]{1,0:T(8,128)(2,1)S(1)}, f32[16,48,1024]{2,1,0:T(8,128)}) fusion(f32[16,48,1024]{2,1,0:T(8,128)S(1)} %fusion.4, bf16[1,1,1024,3584]{3,2,1,0:T(8,128)(2,1)} %param.19, bf16[16,1,48,3584]{3,2,1,0:T(8,128)(2,1)} %all-to-all-done.2), kind=kOutput, calls=%fused_computation.38 | convolution fusion | flops 5643435008 | bytes 19138048 | tf_op jit(solution)/shard_map/secd,efd->secf/dot_general | solution.py:96
  319.4 79.2 %all-to-all-done = bf16[16,1,48,3584]{3,2,1,0:T(8,128)(2,1)} async-done(((bf16[16,1,48,3584]{3,2,1,0:T(8,128)(2,1)}), bf16[16,1,48,3584]{3,2,1,0:T(8,128)(2,1)}, u32[]{:S(2)}, u32[]{:S(2)}) %all-to-all-start) | async-done | bytes 5505056 | tf_op jit(solution)/shard_map/all_to_all | solution.py:75
  398.6 25.2 %all-to-all-start.5 = ((bf16[16,1,48]{2,1,0:T(2,128)(2,1)}), bf16[16,1,48]{2,1,0:T(2,128)(2,1)S(1)}, u32[]{:S(2)}, u32[]{:S(2)}) async-start(bf16[16,1,48]{2,1,0:T(2,128)(2,1)} %copy.93), calls=%async_computation.5 | async-start | bytes 16384 | tf_op jit(solution)/shard_map/all_to_all | solution.py:109
  423.8 13.1 %fusion.18 = bf16[16,1,48,3584]{3,2,1,0:T(8,128)(2,1)} fusion(bf16[1,1,3584,1024]{3,2,1,0:T(8,128)(2,1)} %param.18, f32[16,48,1024]{2,1,0:T(8,128)} %get-tuple-element.12, f32[16,48,1024]{2,1,0:T(8,128)} %copy-done.11), kind=kOutput, calls=%fused_computation.26 | convolution fusion | flops 5646974976 | bytes 19136512 | tf_op jit(solution)/shard_map/secf,edf->secd/dot_general | solution.py:104
  436.9 6.9 all-to-all-start.4
  443.9 10.2 %fusion.38 = bf16[16,1,48,1024]{3,2,0,1:T(8,128)(2,1)S(1)} fusion(bf16[1,1,3584,1024]{3,2,1,0:T(8,128)(2,1)} %param.18, bf16[16,1,48,3584]{3,2,1,0:T(8,128)(2,1)} %all-to-all-done), kind=kOutput, calls=%fused_computation.53 | convolution fusion | flops 5641076736 | bytes 14417920 | tf_op jit(solution)/shard_map/secd,edf->secf/dot_general | solution.py:73
  454.0 10.7 %fusion.21 = bf16[16,1,48,3584]{3,2,1,0:T(8,128)(2,1)} fusion(bf16[1,1,1024,3584]{3,2,1,0:T(8,128)(2,1)} %param.19, bf16[16,1,48,1024]{3,2,0,1:T(8,128)(2,1)S(1)} %fusion.38), kind=kOutput, calls=%fused_computation.27 | convolution fusion | flops 5639897088 | bytes 14417920 | tf_op jit(solution)/shard_map/secf,efd->secd/dot_general | solution.py:81
  464.7 79.9 %all-to-all-done.4 = bf16[16,1,48,3584]{3,2,1,0:T(8,128)(2,1)} async-done(((bf16[16,1,48,3584]{3,2,1,0:T(8,128)(2,1)}), bf16[16,1,48,3584]{3,2,1,0:T(8,128)(2,1)}, u32[]{:S(2)}, u32[]{:S(2)}) %all-to-all-start.4) | async-done | bytes 5505056 | tf_op jit(solution)/shard_map/all_to_all | solution.py:108
  544.6 25.1 %all-to-all-start.1 = ((bf16[16,1,48,3584]{3,2,1,0:T(8,128)(2,1)}), bf16[16,1,48,3584]{3,2,1,0:T(8,128)(2,1)}, u32[]{:S(2)}, u32[]{:S(2)}) async-start(bf16[16,1,48,3584]{3,2,1,0:T(8,128)(2,1)} %fusion.21), calls=%async_computation.1 | async-start | bytes 11010048 | tf_op jit(solution)/shard_map/all_to_all | solution.py:80
  570.5 3.9 gather_fusion.5
  575.0 3.5 gather_fusion.2
  579.4 3.9 gather_fusion.3
  585.0 163.3 %all-reduce.3.cloned.1.call-done = bf16[16,3584]{1,0:T(8,128)(2,1)} async-done(((bf16[16,3584]{1,0:T(8,128)(2,1)}), bf16[16,3584]{1,0:T(8,128)(2,1)}) %all-reduce.3.cloned.1.call-update) | async-done | bytes 114704
  748.3 2.1 bitcast_convert_fusion
  750.4 11.1 %gather_fusion.1 = bf16[512,3584]{1,0:T(8,128)(2,1)} fusion(bf16[768,3584]{1,0:T(8,128)(2,1)} %bitcast.57, s32[1024]{0:T(1024)S(1)} %pad_clamp_fusion), kind=kCustom, calls=%fused_computation.6 | custom fusion | bytes 7342080 | tf_op jit(solution)/shard_map/gather | solution.py:115
  761.5 5.1 fusion
  767.5 11.5 %gather_fusion = bf16[512,3584]{1,0:T(8,128)(2,1)} fusion(bf16[768,3584]{1,0:T(8,128)(2,1)} %bitcast.25, s32[1024]{0:T(1024)S(1)} %pad_clamp_fusion.2), kind=kCustom, calls=%fused_computation.5 | custom fusion | bytes 7342080 | tf_op jit(solution)/shard_map/gather | solution.py:110
  779.0 5.1 fusion.1
  (102 shorter events, 14.2 us)
Async XLA Ops:
  7.2 563.0 %copy-start = (bf16[1,16,3584]{2,1,0:T(8,128)(2,1)S(1)}, bf16[1,16,3584]{2,1,0:T(8,128)(2,1)}, u32[]{:S(2)}) copy-start(bf16[1,16,3584]{2,1,0:T(8,128)(2,1)} %param.17) | copy-start | bytes 344068
  10.6 0.6 copy-start.7
  16.6 5.4 copy-start.1
  165.8 4.8 copy-start.6
  165.8 9.2 %copy-start.4 = (bf16[1,64,3584]{2,1,0:T(8,128)(2,1)S(1)}, bf16[1,64,3584]{2,1,0:T(8,128)(2,1)}, u32[]{:S(2)}) copy-start(bf16[1,64,3584]{2,1,0:T(8,128)(2,1)} %param.12) | copy-start | bytes 1376260
  165.8 105.5 %all-to-all-start.2 = ((bf16[16,1,48,3584]{3,2,1,0:T(8,128)(2,1)}), bf16[16,1,48,3584]{3,2,1,0:T(8,128)(2,1)}, u32[]{:S(2)}, u32[]{:S(2)}) async-start(bf16[16,1,48,3584]{3,2,1,0:T(8,128)(2,1)} %bitcast.270), calls=%async_computation.2 | async-start | bytes 11010048 | tf_op jit(solution)/shard_map/all_to_all | solution.py:98
  271.3 127.3 %all-to-all-start = ((bf16[16,1,48,3584]{3,2,1,0:T(8,128)(2,1)}), bf16[16,1,48,3584]{3,2,1,0:T(8,128)(2,1)}, u32[]{:S(2)}, u32[]{:S(2)}) async-start(bf16[16,1,48,3584]{3,2,1,0:T(8,128)(2,1)} %bitcast.271), calls=%async_computation | async-start | bytes 11010048 | tf_op jit(solution)/shard_map/all_to_all | solution.py:75
  306.3 12.5 %copy-start.11 = (f32[16,48,1024]{2,1,0:T(8,128)}, f32[16,48,1024]{2,1,0:T(8,128)S(1)}, u32[]{:S(2)}) copy-start(f32[16,48,1024]{2,1,0:T(8,128)S(1)} %fusion.4) | copy-start | bytes 9437188
  398.6 38.3 %all-to-all-start.5 = ((bf16[16,1,48]{2,1,0:T(2,128)(2,1)}), bf16[16,1,48]{2,1,0:T(2,128)(2,1)S(1)}, u32[]{:S(2)}, u32[]{:S(2)}) async-start(bf16[16,1,48]{2,1,0:T(2,128)(2,1)} %copy.93), calls=%async_computation.5 | async-start | bytes 16384 | tf_op jit(solution)/shard_map/all_to_all | solution.py:109
  436.9 107.7 %all-to-all-start.4 = ((bf16[16,1,48,3584]{3,2,1,0:T(8,128)(2,1)}), bf16[16,1,48,3584]{3,2,1,0:T(8,128)(2,1)}, u32[]{:S(2)}, u32[]{:S(2)}) async-start(bf16[16,1,48,3584]{3,2,1,0:T(8,128)(2,1)} %fusion.18), calls=%async_computation.4 | async-start | bytes 11010048 | tf_op jit(solution)/shard_map/all_to_all | solution.py:108
  464.7 105.3 %copy-start.5 = (s32[1,64,8]{1,2,0:T(8,128)S(1)}, s32[1,64,8]{1,2,0:T(8,128)}, u32[]{:S(2)}) copy-start(s32[1,64,8]{1,2,0:T(8,128)} %param.15) | copy-start | bytes 6148
  464.7 105.5 %copy-start.3 = (bf16[1,64,3584]{2,1,0:T(8,128)(2,1)S(1)}, bf16[1,64,3584]{2,1,0:T(8,128)(2,1)}, u32[]{:S(2)}) copy-start(bf16[1,64,3584]{2,1,0:T(8,128)(2,1)} %param.14) | copy-start | bytes 1376260
  544.6 222.9 %all-to-all-start.1 = ((bf16[16,1,48,3584]{3,2,1,0:T(8,128)(2,1)}), bf16[16,1,48,3584]{3,2,1,0:T(8,128)(2,1)}, u32[]{:S(2)}, u32[]{:S(2)}) async-start(bf16[16,1,48,3584]{3,2,1,0:T(8,128)(2,1)} %fusion.21), calls=%async_computation.1 | async-start | bytes 11010048 | tf_op jit(solution)/shard_map/all_to_all | solution.py:80
  569.7 178.6 %all-reduce.3.cloned.1.call-start = ((), (), s32[]{:S(2)}) async-start(), calls=%async_computation.6 | async-start | bytes 229376
  570.5 4.1 copy-start.8
  579.1 4.4 collective-permute-start
  579.4 4.9 copy-start.10
  779.0 6.0 copy-start.2
  779.0 6.0 copy-start.9
Sparse Core Ops, SparseCore 0:
  584.3 163.9 all-reduce.2
where the time goes:
time: 801 us; the launch traced here: 793 us
  waiting for transfers between devices  407 us (51%)
  blocking collectives  131 us (16%)
  starting transfers between devices  87.7 us (11%)
  local copies, waits for them, and re-layouts  60 us (7%)
  matrix products  57.8 us (7%)
  other arithmetic  34.9 us (4%)
  between operations  14.9 us (2%)
    unnamed x2, waiting for transfers between devices  163 us
    all_to_all x1, blocking collectives, on_device(): lax.all_to_all(send_b, 'expert', split_axis=0, concat_axis=0, tiled=True)  131 us
    all_to_all x1, waiting for transfers between devices, on_device(): lax.all_to_all(send_grad, 'expert', split_axis=0, concat_axis=0, tiled=True)  85 us
    all_to_all x1, waiting for transfers between devices, on_device(): lax.all_to_all(lifted, 'expert', split_axis=0, concat_axis=0, tiled=True)  79.9 us
    all_to_all x1, waiting for transfers between devices, on_device(): lax.all_to_all(send_a, 'expert', split_axis=0, concat_axis=0, tiled=True)  79.2 us
    all_to_all x1, starting transfers between devices, on_device(): lax.all_to_all(send_a, 'expert', split_axis=0, concat_axis=0, tiled=True)  25.3 us
    all_to_all x1, starting transfers between devices, on_device(): lax.all_to_all(score, 'expert', split_axis=0, concat_axis=0, tiled=True)  25.2 us
    all_to_all x1, starting transfers between devices, on_device(): lax.all_to_all(jnp.einsum('secf,efd->secd', active, down_local, preferred...  25.1 us
  transfers between devices with their start and end apart: 7, of which 4 were waited for; matrix products, arithmetic and copies ran while one was open for 13% of the time, Pallas kernels for 0%

commit v1 on v0

v1 whole, which is shorter than its diff:
```python
import jax
import jax.numpy as jnp
from jax import lax
from jax.sharding import PartitionSpec as P

ROUTED_SCALE = 2.5
EPSILON = 1e-06


def partner(block, axis, bit):
    count = lax.axis_size(axis)
    route = []
    for low in range(count):
        high = low | 1 << bit
        if high != low and high < count:
            route += [(low, high), (high, low)]
    return lax.ppermute(block, axis, route)


def gather(block):
    return lax.all_gather(block, "expert", axis=0, tiled=True)


def prepare(hidden, routes, router_segment):
    expert_count = router_segment.shape[0]
    hidden32 = hidden.astype(jnp.float32)
    rinv = lax.rsqrt(jnp.mean(hidden32 * hidden32, axis=-1, keepdims=True) + EPSILON)
    normed = (hidden32 * rinv).astype(jnp.bfloat16)
    logits = jnp.einsum("td,ed->te", normed, router_segment, preferred_element_type=jnp.float32)
    chosen = jnp.any(
        routes[:, :, None] == jnp.arange(expert_count, dtype=jnp.int32)[None, None, :], axis=1
    )
    affinity = jnp.where(chosen, jax.nn.sigmoid(logits), 0.0)
    return (hidden32, rinv, normed, affinity)


def on_device(hidden_a, routes_a, hidden_b, routes_b, grad_out_b, router, w_up, w_down):
    n_expert = lax.axis_size("expert")
    me = lax.axis_index("expert")
    tok_count = hidden_a.shape[1]
    router_segment = router[0]
    expert_count = router_segment.shape[0]
    local_count = w_up.shape[1]
    hidden32_a, rinv_a, normed_a, affinity_a = prepare(hidden_a[0], routes_a[0], router_segment)
    hidden32_b, rinv_b, normed_b, affinity_b = prepare(hidden_b[0], routes_b[0], router_segment)
    grad_out = grad_out_b[0]
    affinities = gather(jnp.concatenate([affinity_a, affinity_b], axis=1))
    rows_a = gather(normed_a)
    rows_b = gather(normed_b)
    rows_g = gather(grad_out)
    aff_a, aff_b = affinities[:, :expert_count], affinities[:, expert_count:]
    total_b = jnp.sum(aff_b, axis=1, keepdims=True)
    weight_a = aff_a / jnp.sum(aff_a, axis=1, keepdims=True)
    weight_b = aff_b / total_b

    def column(table, local):
        return lax.dynamic_slice_in_dim(table, me * local_count + local, 1, axis=1)

    sum_a = 0.0
    sum_b = 0.0
    scores = []
    for local in range(local_count):
        up, down = w_up[0, local], w_down[0, local]
        pre = jnp.dot(rows_a, up, preferred_element_type=jnp.float32)
        active = jax.nn.silu(pre).astype(jnp.bfloat16)
        out = jnp.dot(active, down, preferred_element_type=jnp.float32)
        sum_a = sum_a + out * column(weight_a, local)
    for local in range(local_count):
        up, down = w_up[0, local], w_down[0, local]
        pre = jnp.dot(rows_b, up, preferred_element_type=jnp.float32)
        back = jnp.einsum("td,fd->tf", rows_g, down, preferred_element_type=jnp.float32)
        sig = jax.nn.sigmoid(pre)
        scores.append(jnp.sum(back * (pre * sig), axis=-1))
        inner = (back * (sig * (1.0 + pre * (1.0 - sig)))).astype(jnp.bfloat16)
        lifted = jnp.einsum("tf,df->td", inner, up, preferred_element_type=jnp.float32)
        sum_b = sum_b + lifted * column(weight_b, local)
    mixed = lax.psum_scatter(
        sum_a.astype(jnp.bfloat16), "expert", scatter_dimension=0, tiled=True
    ).astype(jnp.float32)
    layer_out = (hidden32_a + ROUTED_SCALE * mixed).astype(jnp.bfloat16)

    score = gather(jnp.stack(scores)).T
    score = jnp.where(aff_b > 0.0, score, 0.0)
    gate_grad = ROUTED_SCALE * score
    logit_grad = (
        aff_b
        * (1.0 - aff_b)
        * (gate_grad - jnp.sum(gate_grad * weight_b, axis=1, keepdims=True))
        / total_b
    )
    own_columns = lax.dynamic_slice_in_dim(logit_grad, me * local_count, local_count, axis=1)
    own_term = jnp.dot(
        own_columns.T, rows_b.astype(jnp.float32), precision=lax.Precision.HIGHEST
    )
    mirrored = own_term
    for bit in range(lax.axis_size("pipe").bit_length() - 1):
        mirrored = partner(mirrored, "pipe", bit)
    router_grad = own_term + mirrored

    dense = lax.dynamic_slice_in_dim(logit_grad, me * tok_count, tok_count, axis=0)
    lifted_sum = lax.psum_scatter(
        sum_b.astype(jnp.bfloat16), "expert", scatter_dimension=0, tiled=True
    ).astype(jnp.float32)
    normed_grad = ROUTED_SCALE * lifted_sum + jnp.dot(
        dense, router_segment.astype(jnp.float32), precision=lax.Precision.HIGHEST
    )
    mean_term = jnp.mean(normed_grad * hidden32_b, axis=-1, keepdims=True)
    grad_in = (
        grad_out.astype(jnp.float32) + rinv_b * normed_grad - hidden32_b * rinv_b**3 * mean_term
    )
    return (layer_out[None], grad_in.astype(jnp.bfloat16)[None], router_grad[None])


def solution(mesh):
    placed = (
        P("pipe", "expert", None),
        P("pipe", "expert", None),
        P("pipe", "expert", None),
        P("pipe", "expert", None),
        P("pipe", "expert", None),
        P("pipe", None, None),
        P("pipe", "expert", None, None),
        P("pipe", "expert", None, None),
    )
    return jax.shard_map(
        on_device,
        mesh=mesh,
        in_specs=placed,
        out_specs=(P("pipe", "expert", None), P("pipe", "expert", None), P("pipe", "expert", None)),
        check_vma=False,
    )
```

time: 801 us -> 656 us (0.82)
  starting transfers between devices: 87.7 us -> 0.42 us
  local copies, waits for them, and re-layouts: 60 us -> 0.34 us
  waiting for transfers between devices: 407 us -> 464 us
  blocking collectives: 131 us -> 85.1 us
  other arithmetic: 34.9 us -> 11.5 us
  matrix products: 57.8 us -> 79.9 us
    reduce_scatter x0 -> x2, waiting for transfers between devices: none -> 283 us  [the longest x1 158 us: on_device(): lax.psum_scatter(sum_a.astype(jnp.bfloat16), 'expert', scatter_dimension=...]
    all_to_all x5 -> x0, waiting for transfers between devices: 244 us -> none  [the longest x1 85 us: on_device(): lax.all_to_all(send_grad, 'expert', split_axis=0, concat_axis=0, tiled=True)]
    all_gather x0 -> x3, waiting for transfers between devices: none -> 179 us  [gather(): return lax.all_gather(block, 'expert', axis=0, tiled=True)]
    unnamed x2 -> x5, waiting for transfers between devices: 163 us -> 0.76 us
    all_to_all x1 -> x0, blocking collectives: 131 us -> none  [on_device(): lax.all_to_all(send_b, 'expert', split_axis=0, concat_axis=0, tiled=True)]
    all_to_all x5 -> x0, starting transfers between devices: 87.4 us -> none  [the longest x1 25.3 us: on_device(): lax.all_to_all(send_a, 'expert', split_axis=0, concat_axis=0, tiled=True)]
    all_gather x0 -> x2, blocking collectives: none -> 85.1 us  [gather(): return lax.all_gather(block, 'expert', axis=0, tiled=True)]
    gather x16 -> x0, local copies, waits for them, and re-layouts: 50.9 us -> none  [the longest x1 11.5 us: on_device(): return_a.reshape(-1, model_dim)[slot_a]]
  transfers between devices with their start and end apart: 7 -> 6, of which waited for: 4 -> 6; matrix products, arithmetic and copies ran while one was open for 13% -> 13% of each run, Pallas kernels for 0% -> 0%
where the time goes in v1:
time: 656 us; the launch traced here: 655 us
  waiting for transfers between devices  464 us (71%)
  blocking collectives  85.1 us (13%)
  matrix products  79.9 us (12%)
  between operations  13.9 us (2%)
  other arithmetic  11.5 us (2%)
    all_gather x3, waiting for transfers between devices, gather(): return lax.all_gather(block, 'expert', axis=0, tiled=True)  179 us
    reduce_scatter x1, waiting for transfers between devices, on_device(): lax.psum_scatter(sum_a.astype(jnp.bfloat16), 'expert', scatter_dimension=...  158 us
    reduce_scatter x1, waiting for transfers between devices, on_device(): lax.psum_scatter(sum_b.astype(jnp.bfloat16), 'expert', scatter_dimension=...  125 us
    all_gather x2, blocking collectives, gather(): return lax.all_gather(block, 'expert', axis=0, tiled=True)  85.1 us
    dot_general x1, matrix products, on_device(): jnp.einsum('tf,df->td', inner, up, preferred_element_type=jnp.float32)  16.5 us
    dot_general x1, matrix products, on_device(): jnp.einsum('td,fd->tf', rows_g, down, preferred_element_type=jnp.float32)  14.6 us
    dot_general x1, matrix products, on_device(): pre = jnp.dot(rows_b, up, preferred_element_type=jnp.float32)  13.5 us
  transfers between devices with their start and end apart: 6, of which 6 were waited for; matrix products, arithmetic and copies ran while one was open for 13% of the time, Pallas kernels for 0%

profile of v1, /device:TPU:0, one launch (start us, length us, event | category | flops | bytes accessed | tf_op | source)
XLA Modules:
  0.0 654.9 jit_solution(2670223846619747386)
XLA Ops:
  7.2 1.2 fusion.27
  8.5 1.9 fusion.28
  10.4 0.0 all-gather.11.cloned.1.call-start
  10.5 0.7 all-gather.11.cloned.1.call-update
  11.2 1.2 fusion.34
  12.4 1.9 fusion.35
  14.4 0.0 reduce-scatter.5.cloned.1.call-start
  14.5 0.7 fusion.53
  15.2 0.7 fusion.52
  15.9 1.3 fusion.22
  17.2 1.4 fusion.26
  18.6 45.7 %all-gather.2 = f32[16,64,32]{1,2,0:T(8,128)S(1)} all-gather(f32[1,64,32]{1,2,0:T(8,128)S(1)} %maximum_bitcast_fusion), channel_id=1, replica_groups=mesh['pipe'=2,'expert'=16] {'expert'}, dimensions={0}, use_global_device_ids=true | all-gather | bytes 139264 | tf_op jit(solution)/shard_map/all_gather | solution.py:21
  64.2 0.2 copy.34
  64.4 0.1 reshape.69
  64.5 54.4 %all-gather.9.cloned.1.call-done = bf16[1024,3584]{1,0:T(8,128)(2,1)} async-done(((bf16[64,3584]{1,0:T(8,128)(2,1)}), bf16[1024,3584]{1,0:T(8,128)(2,1)}) %all-gather.9.cloned.1.call-update) | async-done | bytes 7340048 | tf_op jit(solution)/shard_map/all_gather | solution.py:21
  119.0 13.5 %fusion.5 = f32[1024,1024]{1,0:T(8,128)} fusion(bf16[1024,3584]{1,0:T(8,128)(2,1)} %all-gather.9.cloned.1.call-done, bf16[1,1,3584,1024]{3,2,1,0:T(8,128)(2,1)} %param.14), kind=kOutput, calls=%fused_computation.7 | convolution fusion | flops 7516192768 | bytes 18874368 | tf_op jit(solution)/shard_map/dot_general | solution.py:70
  132.5 90.4 %all-gather.11.cloned.1.call-done = bf16[1,1024,3584]{2,1,0:T(8,128)(2,1)} async-done(((bf16[1,64,3584]{2,1,0:T(8,128)(2,1)}), bf16[1,1024,3584]{2,1,0:T(8,128)(2,1)}) %all-gather.11.cloned.1.call-update) | async-done | bytes 7340048 | tf_op jit(solution)/shard_map/all_gather | solution.py:21
  222.8 14.6 %multiply_reduce_fusion = (f32[1024]{0:T(1024)S(1)}, f32[1024,1024]{1,0:T(8,128)}) fusion(f32[1024,1024]{1,0:T(8,128)} %fusion.5, bf16[1,1,1024,3584]{3,2,1,0:T(8,128)(2,1)} %param.15, bf16[1,1024,3584]{2,1,0:T(8,128)(2,1)} %all-gather.11.cloned.1.call-done), kind=kOutput, calls=%fused_computation.12 | convolution fusion | flops 7522483200 | bytes 23072768 | tf_op jit(solution)/shard_map/td,fd->tf/dot_general | solution.py:71
  237.4 39.4 %all-gather.1 = f32[16384]{0:T(1024)S(1)} all-gather(f32[1024]{0:T(1024)S(1)} %get-tuple-element.10), channel_id=3, replica_groups=mesh['pipe'=2,'expert'=16] {'expert'}, dimensions={0}, use_global_device_ids=true | all-gather | bytes 69632 | tf_op jit(solution)/shard_map/all_gather | solution.py:21
  276.9 16.5 %multiply_convert_fusion = bf16[1024,3584]{1,0:T(8,128)(2,1)} fusion(bf16[1,1,3584,1024]{3,2,1,0:T(8,128)(2,1)} %param.14, f32[1024]{0:T(1024)S(1)} %bitcast.109, f32[1024,1024]{1,0:T(8,128)} %get-tuple-element.11, f32[1024,1024]{1,0:T(8,128)} %fusion.5), kind=kOutput, calls=%fused_computation | convolution fusion | flops 7532969984 | bytes 23072768 | tf_op jit(solution)/shard_map/tf,df->td/dot_general | solution.py:75
  293.4 0.2 reduce-scatter.3.cloned.1.call-start
  293.7 34.1 %all-gather.7.cloned.1.call-done = bf16[1024,3584]{1,0:T(8,128)(2,1)} async-done(((bf16[64,3584]{1,0:T(8,128)(2,1)}), bf16[1024,3584]{1,0:T(8,128)(2,1)}) %all-gather.7.cloned.1.call-update) | async-done | bytes 7340048 | tf_op jit(solution)/shard_map/all_gather | solution.py:21
  327.8 12.7 %multiply_convert_fusion.3 = bf16[1024,1024]{1,0:T(8,128)(2,1)S(1)} fusion(bf16[1024,3584]{1,0:T(8,128)(2,1)} %all-gather.7.cloned.1.call-done, bf16[1,1,3584,1024]{3,2,1,0:T(8,128)(2,1)} %param.14), kind=kOutput, calls=%fused_computation.15 | convolution fusion | flops 7521435648 | bytes 16777216 | tf_op jit(solution)/shard_map/dot_general | solution.py:64
  340.5 12.9 %multiply_convert_fusion.1 = bf16[1024,3584]{1,0:T(8,128)(2,1)} fusion(bf16[1024,1024]{1,0:T(8,128)(2,1)S(1)} %multiply_convert_fusion.3, bf16[1,1,1024,3584]{3,2,1,0:T(8,128)(2,1)} %param.15, f32[1024]{0:T(1024)S(1)} %bitcast.106), kind=kOutput, calls=%fused_computation.1 | convolution fusion | flops 7523532800 | bytes 16781312 | tf_op jit(solution)/shard_map/dot_general | solution.py:66
  353.5 5.2 fusion.55
  358.7 1.2 collective-permute-done
  359.9 0.6 add_bitcast_fusion
  360.5 124.6 %reduce-scatter.5.cloned.1.call-done = bf16[64,3584]{1,0:T(8,128)(2,1)} async-done(((bf16[1024,3584]{1,0:T(8,128)(2,1)}), bf16[64,3584]{1,0:T(8,128)(2,1)}) %reduce-scatter.5.cloned.1.call-update) | async-done | bytes 458768 | tf_op jit(solution)/shard_map/reduce_scatter | solution.py:101
  485.1 1.9 fusion.32
  487.0 1.1 fusion.43
  488.1 158.4 %reduce-scatter.3.cloned.1.call-done = bf16[64,3584]{1,0:T(8,128)(2,1)} async-done(((bf16[1024,3584]{1,0:T(8,128)(2,1)}), bf16[64,3584]{1,0:T(8,128)(2,1)}) %reduce-scatter.3.cloned.1.call-update) | async-done | bytes 458768 | tf_op jit(solution)/shard_map/reduce_scatter | solution.py:77
  646.5 1.9 fusion.40
  (25 shorter events, 0.4 us)
Async XLA Ops:
  7.2 8.7 %copy-start = (bf16[1,16,3584]{2,1,0:T(8,128)(2,1)S(1)}, bf16[1,16,3584]{2,1,0:T(8,128)(2,1)}, u32[]{:S(2)}) copy-start(bf16[1,16,3584]{2,1,0:T(8,128)(2,1)} %param.13) | copy-start | bytes 344068
  7.2 111.8 %all-gather.9.cloned.1.call-start = ((), (), s32[]{:S(2)}) async-start(), calls=%async_computation.4 | async-start | bytes 7798784 | tf_op jit(solution)/shard_map/all_gather | solution.py:21
  10.4 212.4 %all-gather.11.cloned.1.call-start = ((), (), s32[]{:S(2)}) async-start(), calls=%async_computation.6 | async-start | bytes 7798784 | tf_op jit(solution)/shard_map/all_gather | solution.py:21
  11.2 316.6 %all-gather.7.cloned.1.call-start = ((), (), s32[]{:S(2)}) async-start(), calls=%async_computation.2 | async-start | bytes 7798784 | tf_op jit(solution)/shard_map/all_gather | solution.py:21
  14.4 470.7 %reduce-scatter.5.cloned.1.call-start = ((), (), s32[]{:S(2)}) async-start(), calls=%async_computation.5 | async-start | bytes 7798784 | tf_op jit(solution)/shard_map/reduce_scatter | solution.py:101
  293.4 353.1 %reduce-scatter.3.cloned.1.call-start = ((), (), s32[]{:S(2)}) async-start(), calls=%async_computation.3 | async-start | bytes 7798784 | tf_op jit(solution)/shard_map/reduce_scatter | solution.py:77
  353.4 131.7 %copy-start.1 = (bf16[1,64,3584]{2,1,0:T(8,128)(2,1)S(1)}, bf16[1,64,3584]{2,1,0:T(8,128)(2,1)}, u32[]{:S(2)}) copy-start(bf16[1,64,3584]{2,1,0:T(8,128)(2,1)} %param.10) | copy-start | bytes 1376260
  353.4 133.6 %copy-start.3 = (bf16[1,64,3584]{2,1,0:T(8,128)(2,1)S(1)}, bf16[1,64,3584]{2,1,0:T(8,128)(2,1)}, u32[]{:S(2)}) copy-start(bf16[1,64,3584]{2,1,0:T(8,128)(2,1)} %param.12) | copy-start | bytes 1376260
  353.4 293.0 %copy-start.2 = (bf16[1,64,3584]{2,1,0:T(8,128)(2,1)S(1)}, bf16[1,64,3584]{2,1,0:T(8,128)(2,1)}, u32[]{:S(2)}) copy-start(bf16[1,64,3584]{2,1,0:T(8,128)(2,1)} %param.8) | copy-start | bytes 1376260
  358.7 1.2 collective-permute-start
Sparse Core Ops, SparseCore 0:
  11.2 107.6 all-gather.8
  121.7 101.1 all-gather.10
  226.1 101.6 all-gather.6
  330.0 155.1 reduce-scatter.4
  487.3 159.1 reduce-scatter.2

commit v2 on v1

--- a/solution.py
+++ b/solution.py
@@ -1,6 +1,10 @@
+import functools
+
 import jax
 import jax.numpy as jnp
 from jax import lax
+from jax.experimental import pallas as pl
+from jax.experimental.pallas import tpu as pltpu
 from jax.sharding import PartitionSpec as P
 
 ROUTED_SCALE = 2.5
@@ -17,8 +21,294 @@
     return lax.ppermute(block, axis, route)
 
 
-def gather(block):
-    return lax.all_gather(block, "expert", axis=0, tiled=True)
+MESH = pl.DeviceIdType.MESH
+DMA = pltpu.SemaphoreType.DMA
+PLANE = 4
+
+
+def remote(src, dst, send_sem, recv_sem, target):
+    return pltpu.make_async_remote_copy(
+        src_ref=src,
+        dst_ref=dst,
+        send_sem=send_sem,
+        recv_sem=recv_sem,
+        device_id={"expert": target},
+        device_id_type=MESH,
+    )
+
+
+def place():
+    me = lax.axis_index("expert")
+    z, y, x = me // PLANE, (me // 2) % 2, me % 2
+    return (me, z, y, x, me + 1 - 2 * x, me + 2 - 4 * y)
+
+
+def greet(planes):
+    me, z, y, x, x_near, y_near = place()
+    barrier = pltpu.get_barrier_semaphore()
+    pl.semaphore_signal(barrier, inc=1, device_id={"expert": x_near}, device_id_type=MESH)
+    pl.semaphore_signal(barrier, inc=1, device_id={"expert": y_near}, device_id_type=MESH)
+
+    @pl.when(z < planes - 1)
+    def _():
+        pl.semaphore_signal(barrier, inc=1, device_id={"expert": me + PLANE}, device_id_type=MESH)
+
+    @pl.when(z > 0)
+    def _():
+        pl.semaphore_signal(barrier, inc=1, device_id={"expert": me - PLANE}, device_id_type=MESH)
+
+    ends = jnp.where(z == 0, 1, 0) + jnp.where(z == planes - 1, 1, 0)
+    pl.semaphore_wait(barrier, 4 - ends)
+
+
+def gather_kernel(count, planes, *refs):
+    ins, outs = refs[:count], refs[count : 2 * count]
+    own_sem, up_s, down_s, z_r, x_s, x_r, y_s, y_r, d_s, d_r = refs[2 * count :]
+    me, z, y, x, x_near, y_near = place()
+
+    def up(k, p, src):
+        return remote(src, outs[k].at[p * PLANE + y * 2 + x], up_s.at[k, p], z_r.at[k, p], me + PLANE)
+
+    def down(k, p, src):
+        return remote(src, outs[k].at[p * PLANE + y * 2 + x], down_s.at[k, p], z_r.at[k, p], me - PLANE)
+
+    def to_x(k, p, src):
+        return remote(src, outs[k].at[p * PLANE + y * 2 + x], x_s.at[k, p], x_r.at[k, p], x_near)
+
+    def to_y(k, p, src):
+        return remote(src, outs[k].at[p * PLANE + y * 2 + x], y_s.at[k, p], y_r.at[k, p], y_near)
+
+    def half(k, p, way):
+        if way == 0:
+            ref = outs[k].at[p * PLANE + y * 2 + 1 - x, 0]
+            return remote(ref, ref, d_s.at[k, p, 0], d_r.at[k, p, 0], y_near)
+        ref = outs[k].at[p * PLANE + (1 - y) * 2 + x, 1]
+        return remote(ref, ref, d_s.at[k, p, 1], d_r.at[k, p, 1], x_near)
+
+    def each(d, act):
+        if d == 0:
+            act(z, 0)
+            return
+
+        @pl.when(z >= d)
+        def _():
+            act(z - d, 1)
+
+        @pl.when(z + d < planes)
+        def _():
+            act(z + d, -1)
+
+    def spread(k, p, way, wait):
+        src = ins[k] if way == 0 else outs[k].at[p * PLANE + y * 2 + x]
+
+        def do(copy):
+            copy.wait_send() if wait else copy.start()
+
+        if way != 0 and not wait:
+            up(k, p, src).wait_recv()
+        if way >= 0:
+
+            @pl.when(z < planes - 1)
+            def _():
+                do(up(k, p, src))
+
+        if way <= 0:
+
+            @pl.when(z > 0)
+            def _():
+                do(down(k, p, src))
+
+        do(to_x(k, p, src))
+        do(to_y(k, p, src))
+
+    def relay(k, p, way):
+        to_x(k, p, ins[k]).wait_recv()
+        half(k, p, 0).start()
+        to_y(k, p, ins[k]).wait_recv()
+        half(k, p, 1).start()
+
+    def finish(k, p, way):
+        for route in range(2):
+            half(k, p, route).wait()
+        spread(k, p, way, True)
+
+    greet(planes)
+    for k in range(count):
+        pltpu.make_async_copy(ins[k], outs[k].at[me], own_sem.at[k]).start()
+        each(0, lambda p, way: spread(k, p, way, False))
+    for k in range(count):
+        for d in range(1, planes):
+            each(d, lambda p, way: spread(k, p, way, False))
+            each(d - 1, lambda p, way: relay(k, p, way))
+        each(planes - 1, lambda p, way: relay(k, p, way))
+    for k in range(count):
+        for d in range(planes):
+            each(d, lambda p, way: finish(k, p, way))
+        pltpu.make_async_copy(ins[k], outs[k].at[me], own_sem.at[k]).wait()
+
+
+def gather_all(blocks, collective_id):
+    n = lax.axis_size("expert")
+    planes = n // PLANE
+    count = len(blocks)
+    halved = [b.reshape(2, b.shape[0] // 2, b.shape[1]) for b in blocks]
+    outs = pl.pallas_call(
+        functools.partial(gather_kernel, count, planes),
+        out_shape=[jax.ShapeDtypeStruct((n,) + b.shape, b.dtype) for b in halved],
+        in_specs=[pl.BlockSpec(memory_space=pltpu.VMEM)] * count,
+        out_specs=[pl.BlockSpec(memory_space=pl.ANY)] * count,
+        scratch_shapes=[DMA((count,))] + [DMA((count, planes))] * 7 + [DMA((count, planes, 2))] * 2,
+        compiler_params=pltpu.CompilerParams(collective_id=collective_id, has_side_effects=True),
+    )(*halved)
+    return [o.reshape(n * b.shape[0], b.shape[1]) for o, b in zip(outs, blocks)]
+
+
+def scatter_kernel(planes, part, out, a_r, c_r, b_x, b_y, total, z_r, *sems):
+    ax_s, ax_r, ay_s, ay_r, cx_s, cx_r, cy_s, cy_r, z_s, up_r, down_r = sems
+    me, z, y, x, x_near, y_near = place()
+    rows, cols = part.shape[2:]
+    step = 16
+
+    def slot(p, yy, xx):
+        return p * PLANE + yy * 2 + xx
+
+    def add(dst, *srcs):
+        def body(i, carry):
+            r = pl.ds(pl.multiple_of(i * step, step), step)
+            acc = srcs[0][r, :].astype(jnp.float32)
+            for s in srcs[1:]:
+                acc = acc + s[r, :].astype(jnp.float32)
+            dst[r, :] = acc.astype(dst.dtype)
+            return carry
+
+        lax.fori_loop(0, rows // step, body, 0)
+
+    def diagonal(p):
+        src = slot(p, 1 - y, 1 - x)
+        return (
+            remote(part.at[src, 0], a_r.at[p, 0], ay_s.at[p], ay_r.at[p], y_near),
+            remote(part.at[src, 1], a_r.at[p, 1], ax_s.at[p], ax_r.at[p], x_near),
+        )
+
+    def beside(p):
+        return (
+            remote(b_x.at[p, 0], c_r.at[p, 0, 0], cx_s.at[p, 0], cx_r.at[p, 0], x_near),
+            remote(part.at[slot(p, y, 1 - x), 1], c_r.at[p, 0, 1], cx_s.at[p, 1], cx_r.at[p, 1], x_near),
+            remote(b_y.at[p, 0], c_r.at[p, 1, 1], cy_s.at[p, 0], cy_r.at[p, 0], y_near),
+            remote(part.at[slot(p, 1 - y, x), 0], c_r.at[p, 1, 0], cy_s.at[p, 1], cy_r.at[p, 1], y_near),
+        )
+
+    def rise(p):
+        return remote(total.at[p], z_r.at[0, p], z_s.at[p], up_r.at[p], me + PLANE)
+
+    def sink(p):
+        return remote(total.at[p], z_r.at[1, p], z_s.at[p], down_r.at[p], me - PLANE)
+
+    def each(d, act):
+        if d == 0:
+            act(z, 0)
+            return
+
+        @pl.when(z >= d)
+        def _():
+            act(z - d, -1)
+
+        @pl.when(z + d < planes)
+        def _():
+            act(z + d, 1)
+
+    def first(p, way):
+        for copy in diagonal(p):
+            copy.start()
+        beside(p)[1].start()
+        beside(p)[3].start()
+
+    def second(p, way):
+        to_y, to_x = diagonal(p)
+        to_y.wait_recv()
+        add(b_x.at[p, 0], part.at[slot(p, y, 1 - x), 0], a_r.at[p, 0])
+        beside(p)[0].start()
+        to_x.wait_recv()
+        add(b_y.at[p, 0], part.at[slot(p, 1 - y, x), 1], a_r.at[p, 1])
+        beside(p)[2].start()
+
+    def third(p, way):
+        for copy in beside(p):
+            copy.wait_recv()
+        for h in range(2):
+            add(total.at[p, h], part.at[slot(p, y, x), h], c_r.at[p, 0, h], c_r.at[p, 1, h])
+
+        def take(copy, level):
+            copy.wait_recv()
+            for h in range(2):
+                add(total.at[p, h], total.at[p, h], z_r.at[level, p, h])
+
+        if way >= 0:
+
+            @pl.when(z > 0)
+            def _():
+                take(rise(p), 0)
+
+        if way <= 0:
+
+            @pl.when(z < planes - 1)
+            def _():
+                take(sink(p), 1)
+
+        if way > 0:
+            rise(p).start()
+        if way < 0:
+            sink(p).start()
+        if way == 0:
+            out[...] = total[p]
+
+    def finish(p, way):
+        for copy in diagonal(p) + beside(p):
+            copy.wait_send()
+        if way != 0:
+            rise(p).wait_send()
+
+    greet(planes)
+    order = list(range(planes - 1, -1, -1))
+    for d in order:
+        each(d, first)
+    for i, d in enumerate(order):
+        each(d, second)
+        if i > 0:
+            each(order[i - 1], third)
+    each(0, third)
+    for d in order:
+        each(d, finish)
+
+
+def scatter_sum(part, collective_id):
+    n = lax.axis_size("expert")
+    planes = n // PLANE
+    tokens, cols = part.shape
+    rows = tokens // n // 2
+    half = (rows, cols)
+    kind = part.dtype
+    out = pl.pallas_call(
+        functools.partial(scatter_kernel, planes),
+        out_shape=jax.ShapeDtypeStruct((2,) + half, kind),
+        in_specs=[pl.BlockSpec(memory_space=pltpu.VMEM)],
+        out_specs=pl.BlockSpec(memory_space=pltpu.VMEM),
+        scratch_shapes=[
+            pltpu.VMEM((planes, 2) + half, kind),
+            pltpu.VMEM((planes, 2, 2) + half, kind),
+            pltpu.VMEM((planes, 1) + half, kind),
+            pltpu.VMEM((planes, 1) + half, kind),
+            pltpu.VMEM((planes, 2) + half, kind),
+            pltpu.VMEM((2, planes, 2) + half, kind),
+        ]
+        + [DMA((planes,))] * 4
+        + [DMA((planes, 2))] * 4
+        + [DMA((planes,))] * 3,
+        compiler_params=pltpu.CompilerParams(
+            collective_id=collective_id, has_side_effects=True, vmem_limit_bytes=60 << 20
+        ),
+    )(part.reshape((n, 2) + half))
+    return out.reshape(2 * rows, cols)
 
 
 def prepare(hidden, routes, router_segment):
@@ -44,11 +334,11 @@
     hidden32_a, rinv_a, normed_a, affinity_a = prepare(hidden_a[0], routes_a[0], router_segment)
     hidden32_b, rinv_b, normed_b, affinity_b = prepare(hidden_b[0], routes_b[0], router_segment)
     grad_out = grad_out_b[0]
-    affinities = gather(jnp.concatenate([affinity_a, affinity_b], axis=1))
-    rows_a = gather(normed_a)
-    rows_b = gather(normed_b)
-    rows_g = gather(grad_out)
-    aff_a, aff_b = affinities[:, :expert_count], affinities[:, expert_count:]
+    affinity_ab = jnp.concatenate([affinity_a, affinity_b], axis=1)
+    lanes = -(-2 * expert_count // 128) * 128
+    affinity_ab = jnp.pad(affinity_ab, ((0, 0), (0, lanes - 2 * expert_count)))
+    rows_a, rows_b, rows_g, affinities = gather_all([normed_a, normed_b, grad_out, affinity_ab], 1)
+    aff_a, aff_b = affinities[:, :expert_count], affinities[:, expert_count : 2 * expert_count]
     total_b = jnp.sum(aff_b, axis=1, keepdims=True)
     weight_a = aff_a / jnp.sum(aff_a, axis=1, keepdims=True)
     weight_b = aff_b / total_b
@@ -74,12 +364,13 @@
         inner = (back * (sig * (1.0 + pre * (1.0 - sig)))).astype(jnp.bfloat16)
         lifted = jnp.einsum("tf,df->td", inner, up, preferred_element_type=jnp.float32)
         sum_b = sum_b + lifted * column(weight_b, local)
-    mixed = lax.psum_scatter(
-        sum_a.astype(jnp.bfloat16), "expert", scatter_dimension=0, tiled=True
-    ).astype(jnp.float32)
+    mixed = scatter_sum(sum_a.astype(jnp.bfloat16), 2).astype(jnp.float32)
     layer_out = (hidden32_a + ROUTED_SCALE * mixed).astype(jnp.bfloat16)
 
-    score = gather(jnp.stack(scores)).T
+    flat = jnp.stack(scores).reshape(-1)
+    padded = jnp.pad(flat, (0, -flat.shape[0] % 2048)).reshape(-1, 128)
+    score = gather_all([padded], 4)[0].reshape(n_expert, -1)[:, : flat.shape[0]]
+    score = score.reshape(expert_count, -1).T
     score = jnp.where(aff_b > 0.0, score, 0.0)
     gate_grad = ROUTED_SCALE * score
     logit_grad = (
@@ -98,9 +389,7 @@
     router_grad = own_term + mirrored
 
     dense = lax.dynamic_slice_in_dim(logit_grad, me * tok_count, tok_count, axis=0)
-    lifted_sum = lax.psum_scatter(
-        sum_b.astype(jnp.bfloat16), "expert", scatter_dimension=0, tiled=True
-    ).astype(jnp.float32)
+    lifted_sum = scatter_sum(sum_b.astype(jnp.bfloat16), 3).astype(jnp.float32)
     normed_grad = ROUTED_SCALE * lifted_sum + jnp.dot(
         dense, router_segment.astype(jnp.float32), precision=lax.Precision.HIGHEST
     )

time: 656 us -> 471 us (0.72)
  waiting for transfers between devices: 464 us -> 0.01 us
  Pallas kernels: 0 us -> 376 us
  blocking collectives: 85.1 us -> 0 us
  between operations: 13.9 us -> 0.82 us
    pallas_call x0 -> x4, Pallas kernels: none -> 376 us  [the longest x2 211 us: gather_all(): pl.pallas_call(functools.partial(gather_kernel, count, planes), out_shape...]
    reduce_scatter x2 -> x0, waiting for transfers between devices: 283 us -> none  [the longest x1 158 us: on_device(): lax.psum_scatter(sum_a.astype(jnp.bfloat16), 'expert', scatter_dimension=...]
    all_gather x3 -> x0, waiting for transfers between devices: 179 us -> none  [gather(): return lax.all_gather(block, 'expert', axis=0, tiled=True)]
    all_gather x2 -> x0, blocking collectives: 85.1 us -> none  [gather(): return lax.all_gather(block, 'expert', axis=0, tiled=True)]
  transfers between devices with their start and end apart: 6 -> 1, of which waited for: 6 -> 0; matrix products, arithmetic and copies ran while one was open for 13% -> 10% of each run, Pallas kernels for 0% -> 35%
where the time goes in v2:
time: 471 us
  Pallas kernels  376 us (80%)
  matrix products  78.1 us (17%)
  other arithmetic  12.7 us (3%)
    pallas_call x2, Pallas kernels, gather_all(): pl.pallas_call(functools.partial(gather_kernel, count, planes), out_shape...  211 us
    pallas_call x2, Pallas kernels, scatter_sum(): pl.pallas_call(functools.partial(scatter_kernel, planes), out_shape=jax.S...  165 us
    dot_general x1, matrix products, on_device(): jnp.einsum('tf,df->td', inner, up, preferred_element_type=jnp.float32)  16.3 us
    dot_general x1, matrix products, on_device(): jnp.einsum('td,fd->tf', rows_g, down, preferred_element_type=jnp.float32)  15.6 us
    dot_general x1, matrix products, on_device(): pre = jnp.dot(rows_a, up, preferred_element_type=jnp.float32)  13.8 us
    dot_general x1, matrix products, on_device(): out = jnp.dot(active, down, preferred_element_type=jnp.float32)  12.5 us
    dot_general x1, matrix products, on_device(): pre = jnp.dot(rows_b, up, preferred_element_type=jnp.float32)  11.2 us
  transfers between devices with their start and end apart: 1, of which 0 were waited for; matrix products, arithmetic and copies ran while one was open for 10% of the time, Pallas kernels for 35%

profile of v2, /device:TPU:0, one launch (start us, length us, event | category | flops | bytes accessed | tf_op | source)
XLA Modules:
  0.0 470.7 jit_solution(3749981726496549265)
XLA Ops:
  0.6 1.2 fusion.22
  1.9 0.1 rsqrt.30
  2.0 1.2 multiply_reduce_fusion.1
  3.2 0.1 rsqrt.28
  3.3 0.7 fusion.41
  4.0 0.7 fusion.40
  4.7 1.3 fusion.14
  6.1 1.3 fusion.18
  7.5 0.6 pad.8.clone
  8.1 2.3 multiply_convert_fusion.6
  10.4 193.3 %shard_map.103 = (bf16[16,2,32,3584]{3,2,1,0:T(8,128)(2,1)}, bf16[16,2,32,3584]{3,2,1,0:T(8,128)(2,1)}, bf16[16,2,32,3584]{3,2,1,0:T(8,128)(2,1)}, f32[16,2,32,128]{3,2,1,0:T(8,128)}) custom-call(bf16[2,32,3584]{2,1,0:T(8,128)(2,1)} %get-tuple-element.24.refs_0_, bf16[2,32,3584]{2,1,0:T(8,128)(2,1)} %get-tuple-element.23.refs_1_, ...), custom_call_target="tpu_custom_call" | custom-call | tf_op jit(solution)/shard_map/pallas_call | solution.py:155
  203.7 1.7 slice_reduce_fusion
  205.5 0.2 copy.41
  205.6 11.2 %fusion.4 = f32[1024,1024]{1,0:T(8,128)S(1)} fusion(bf16[1024,3584]{1,0:T(8,128)(2,1)} %bitcast.97, bf16[1,1,3584,1024]{3,2,1,0:T(8,128)(2,1)} %param.14), kind=kOutput, calls=%fused_computation.6 | convolution fusion | flops 7516192768 | bytes 18874368 | tf_op jit(solution)/shard_map/dot_general | solution.py:360
  216.9 15.6 %multiply_reduce_fusion = (f32[1024]{0:T(1024)S(1)}, f32[1024,1024]{1,0:T(8,128)}) fusion(f32[1024,1024]{1,0:T(8,128)S(1)} %fusion.4, bf16[1024,3584]{1,0:T(8,128)(2,1)} %bitcast.116, bf16[1,1,1024,3584]{3,2,1,0:T(8,128)(2,1)} %param.15), kind=kOutput, calls=%fused_computation.11 | convolution fusion | flops 7522483200 | bytes 23072768 | tf_op jit(solution)/shard_map/td,fd->tf/dot_general | solution.py:361
  232.5 0.6 pad_bitcast_fusion.refs_0_
  233.1 17.8 %shard_map.106 = f32[16,2,8,128]{3,2,1,0:T(8,128)} custom-call(f32[2,8,128]{2,1,0:T(8,128)} %pad_bitcast_fusion.refs_0_), custom_call_target="tpu_custom_call" | custom-call | tf_op jit(solution)/shard_map/pallas_call | solution.py:155
  250.9 0.9 copy.48
  251.9 5.1 %fusion.43 = f32[1,3584]{1,0:T(1,128)S(1)} fusion(bf16[1024,3584]{1,0:T(8,128)(2,1)} %bitcast.98, f32[1024,16]{0,1:T(8,128)S(1)} %get-tuple-element.15, s32[]{:T(128)S(6)} %select_n.21), kind=kOutput, calls=%fused_computation.70 | convolution fusion | flops 44040192 | bytes 7358468 | tf_op jit(solution)/shard_map/dot_general | solution.py:383
  257.1 13.8 %multiply_convert_fusion.3 = bf16[1024,1024]{1,0:T(8,128)(2,1)} fusion(bf16[1024,3584]{1,0:T(8,128)(2,1)} %bitcast.115, bf16[1,1,3584,1024]{3,2,1,0:T(8,128)(2,1)} %param.14), kind=kOutput, calls=%fused_computation.14 | convolution fusion | flops 7521435648 | bytes 16777216 | tf_op jit(solution)/shard_map/dot_general | solution.py:354
  270.8 0.2 constant_dynamic-slice_fusion.1
  271.0 0.2 copy.45
  271.3 12.5 %multiply_convert_fusion.1 = bf16[1024,3584]{1,0:T(8,128)(2,1)} fusion(bf16[1024,1024]{1,0:T(8,128)(2,1)} %multiply_convert_fusion.3, bf16[1,1,1024,3584]{3,2,1,0:T(8,128)(2,1)} %param.15, f32[1024]{0:T(1024)S(1)} %bitcast.111), kind=kOutput, calls=%fused_computation.1 | convolution fusion | flops 7523532800 | bytes 16781312 | tf_op jit(solution)/shard_map/dot_general | solution.py:356
  283.8 81.8 %shard_map.104 = bf16[2,32,3584]{2,1,0:T(8,128)(2,1)} custom-call(bf16[16,2,32,3584]{3,2,1,0:T(8,128)(2,1)} %bitcast.100), custom_call_target="tpu_custom_call" | custom-call | tf_op jit(solution)/shard_map/pallas_call | solution.py:291
  365.6 1.1 convert_multiply_fusion.2
  366.7 16.3 %multiply_convert_fusion = bf16[1024,3584]{1,0:T(8,128)(2,1)} fusion(bf16[1,1,3584,1024]{3,2,1,0:T(8,128)(2,1)} %param.14, f32[1024]{0:T(1024)S(1)} %bitcast.114, f32[1024,1024]{1,0:T(8,128)} %get-tuple-element.20, f32[1024,1024]{1,0:T(8,128)} %copy-done.4), kind=kOutput, calls=%fused_computation | convolution fusion | flops 7532969984 | bytes 23072768 | tf_op jit(solution)/shard_map/tf,df->td/dot_general | solution.py:365
  383.1 83.1 %shard_map.105 = bf16[2,32,3584]{2,1,0:T(8,128)(2,1)} custom-call(bf16[16,2,32,3584]{3,2,1,0:T(8,128)(2,1)} %bitcast.99), custom_call_target="tpu_custom_call" | custom-call | tf_op jit(solution)/shard_map/pallas_call | solution.py:291
  466.2 1.1 convert_multiply_fusion.1
  467.3 0.8 fusion.24
  468.1 1.1 fusion.30
  469.2 0.8 fusion.21
  470.1 0.6 add_bitcast_fusion
  (21 shorter events, 0.3 us)
Async XLA Ops:
  0.6 4.1 copy-start
  216.9 15.6 %copy-start.4 = (f32[1024,1024]{1,0:T(8,128)}, f32[1024,1024]{1,0:T(8,128)S(1)}, u32[]{:S(2)}) copy-start(f32[1024,1024]{1,0:T(8,128)S(1)} %fusion.4) | copy-start | bytes 12582916
  257.0 213.1 %collective-permute-start = (f32[1,3584]{1,0:T(1,128)S(1)}, f32[1,3584]{1,0:T(1,128)S(1)}, u32[]{:S(2)}, u32[]{:S(2)}) collective-permute-start(f32[1,3584]{1,0:T(1,128)S(1)} %fusion.43), channel_id=1, source_target_pairs={{0,16},{16,0},{1,17},{17,1},{2,18},{18,2},{3,19},{19,3},{4,20},{20... | collective-permute-start | bytes 43016 | tf_op jit(solution)/shard_map/ppermute | solution.py:21
  383.0 84.2 %copy-start.1 = (bf16[1,64,3584]{2,1,0:T(8,128)(2,1)S(1)}, bf16[1,64,3584]{2,1,0:T(8,128)(2,1)}, u32[]{:S(2)}) copy-start(bf16[1,64,3584]{2,1,0:T(8,128)(2,1)} %param.10) | copy-start | bytes 1376260
  383.0 85.1 %copy-start.3 = (bf16[1,64,3584]{2,1,0:T(8,128)(2,1)S(1)}, bf16[1,64,3584]{2,1,0:T(8,128)(2,1)}, u32[]{:S(2)}) copy-start(bf16[1,64,3584]{2,1,0:T(8,128)(2,1)} %param.12) | copy-start | bytes 1376260
  383.0 86.2 %copy-start.2 = (bf16[1,64,3584]{2,1,0:T(8,128)(2,1)S(1)}, bf16[1,64,3584]{2,1,0:T(8,128)(2,1)}, u32[]{:S(2)}) copy-start(bf16[1,64,3584]{2,1,0:T(8,128)(2,1)} %param.8) | copy-start | bytes 1376260

commit v3 on v2

--- a/solution.py
+++ b/solution.py
@@ -163,7 +163,7 @@
     return [o.reshape(n * b.shape[0], b.shape[1]) for o, b in zip(outs, blocks)]
 
 
-def scatter_kernel(planes, part, out, a_r, c_r, b_x, b_y, total, z_r, *sems):
+def scatter_stages(planes, part, out, a_r, c_r, b_x, b_y, total, z_r, *sems):
     ax_s, ax_r, ay_s, ay_r, cx_s, cx_r, cy_s, cy_r, z_s, up_r, down_r = sems
     me, z, y, x, x_near, y_near = place()
     rows, cols = part.shape[2:]
@@ -204,19 +204,6 @@
     def sink(p):
         return remote(total.at[p], z_r.at[1, p], z_s.at[p], down_r.at[p], me - PLANE)
 
-    def each(d, act):
-        if d == 0:
-            act(z, 0)
-            return
-
-        @pl.when(z >= d)
-        def _():
-            act(z - d, -1)
-
-        @pl.when(z + d < planes)
-        def _():
-            act(z + d, 1)
-
     def first(p, way):
         for copy in diagonal(p):
             copy.start()
@@ -268,47 +255,83 @@
         if way != 0:
             rise(p).wait_send()
 
+    return (first, second, third, finish)
+
+
+def scatter_kernel(planes, count, *refs):
+    parts, outs, rest = refs[:count], refs[count : 2 * count], refs[2 * count :]
+    per = len(rest) // count
+    z = place()[1]
+    stages = [
+        scatter_stages(planes, parts[k], outs[k], *rest[k * per : (k + 1) * per])
+        for k in range(count)
+    ]
+
+    def each(d, act):
+        if d == 0:
+            act(z, 0)
+            return
+
+        @pl.when(z >= d)
+        def _():
+            act(z - d, -1)
+
+        @pl.when(z + d < planes)
+        def _():
+            act(z + d, 1)
+
     greet(planes)
     order = list(range(planes - 1, -1, -1))
-    for d in order:
-        each(d, first)
+    for k in range(count):
+        for d in order:
+            each(d, stages[k][0])
     for i, d in enumerate(order):
-        each(d, second)
+        for k in range(count):
+            each(d, stages[k][1])
         if i > 0:
-            each(order[i - 1], third)
-    each(0, third)
-    for d in order:
-        each(d, finish)
-
-
-def scatter_sum(part, collective_id):
+            for k in range(count):
+                each(order[i - 1], stages[k][2])
+    for k in range(count):
+        each(0, stages[k][2])
+    for k in range(count):
+        for d in order:
+            each(d, stages[k][3])
+
+
+def scatter_sums(parts, collective_id):
     n = lax.axis_size("expert")
     planes = n // PLANE
-    tokens, cols = part.shape
+    tokens, cols = parts[0].shape
     rows = tokens // n // 2
     half = (rows, cols)
-    kind = part.dtype
-    out = pl.pallas_call(
-        functools.partial(scatter_kernel, planes),
-        out_shape=jax.ShapeDtypeStruct((2,) + half, kind),
-        in_specs=[pl.BlockSpec(memory_space=pltpu.VMEM)],
-        out_specs=pl.BlockSpec(memory_space=pltpu.VMEM),
-        scratch_shapes=[
-            pltpu.VMEM((planes, 2) + half, kind),
-            pltpu.VMEM((planes, 2, 2) + half, kind),
-            pltpu.VMEM((planes, 1) + half, kind),
-            pltpu.VMEM((planes, 1) + half, kind),
-            pltpu.VMEM((planes, 2) + half, kind),
-            pltpu.VMEM((2, planes, 2) + half, kind),
-        ]
-        + [DMA((planes,))] * 4
-        + [DMA((planes, 2))] * 4
-        + [DMA((planes,))] * 3,
+    kind = parts[0].dtype
+    count = len(parts)
+    if count > 1 and count * 3 * parts[0].size * kind.itemsize > 56 << 20:
+        return [scatter_sums([part], collective_id + k)[0] for k, part in enumerate(parts)]
+    outs = pl.pallas_call(
+        functools.partial(scatter_kernel, planes, count),
+        out_shape=[jax.ShapeDtypeStruct((2,) + half, kind)] * count,
+        in_specs=[pl.BlockSpec(memory_space=pltpu.VMEM)] * count,
+        out_specs=[pl.BlockSpec(memory_space=pltpu.VMEM)] * count,
+        scratch_shapes=(
+            [
+                pltpu.VMEM((planes, 2) + half, kind),
+                pltpu.VMEM((planes, 2, 2) + half, kind),
+                pltpu.VMEM((planes, 1) + half, kind),
+                pltpu.VMEM((planes, 1) + half, kind),
+                pltpu.VMEM((planes, 2) + half, kind),
+                pltpu.VMEM((2, planes, 2) + half, kind),
+            ]
+            + [DMA((planes,))] * 4
+            + [DMA((planes, 2))] * 4
+            + [DMA((planes,))] * 3
+        )
+        * count,
         compiler_params=pltpu.CompilerParams(
             collective_id=collective_id, has_side_effects=True, vmem_limit_bytes=60 << 20
         ),
-    )(part.reshape((n, 2) + half))
-    return out.reshape(2 * rows, cols)
+    )(*[part.reshape((n, 2) + half) for part in parts])
+    return [out.reshape(2 * rows, cols) for out in outs]
 
 
 def prepare(hidden, routes, router_segment):
@@ -364,7 +387,8 @@
         inner = (back * (sig * (1.0 + pre * (1.0 - sig)))).astype(jnp.bfloat16)
         lifted = jnp.einsum("tf,df->td", inner, up, preferred_element_type=jnp.float32)
         sum_b = sum_b + lifted * column(weight_b, local)
-    mixed = scatter_sum(sum_a.astype(jnp.bfloat16), 2).astype(jnp.float32)
+    sum_ab = scatter_sums([sum_a.astype(jnp.bfloat16), sum_b.astype(jnp.bfloat16)], 2)
+    mixed = sum_ab[0].astype(jnp.float32)
     layer_out = (hidden32_a + ROUTED_SCALE * mixed).astype(jnp.bfloat16)
 
     flat = jnp.stack(scores).reshape(-1)
@@ -389,7 +413,7 @@
     router_grad = own_term + mirrored
 
     dense = lax.dynamic_slice_in_dim(logit_grad, me * tok_count, tok_count, axis=0)
-    lifted_sum = scatter_sum(sum_b.astype(jnp.bfloat16), 3).astype(jnp.float32)
+    lifted_sum = sum_ab[1].astype(jnp.float32)
     normed_grad = ROUTED_SCALE * lifted_sum + jnp.dot(
         dense, router_segment.astype(jnp.float32), precision=lax.Precision.HIGHEST
     )

time: 471 us -> 459 us (0.975)
  Pallas kernels: 376 us -> 364 us
    pallas_call x2 -> x1, Pallas kernels: 165 us -> 153 us  [scatter_sums(): pl.pallas_call(functools.partial(scatter_kernel, planes, count), out_shap...]
  transfers between devices with their start and end apart: 1 -> 1, of which waited for: 0 -> 0; matrix products, arithmetic and copies ran while one was open for 10% -> 10% of each run, Pallas kernels for 35% -> 33%
where the time goes in v3:
time: 459 us; the launch traced here: 458 us
  Pallas kernels  364 us (79%)
  matrix products  77.3 us (17%)
  other arithmetic  12.7 us (3%)
    pallas_call x2, Pallas kernels, gather_all(): pl.pallas_call(functools.partial(gather_kernel, count, planes), out_shape...  211 us
    pallas_call x1, Pallas kernels, scatter_sums(): pl.pallas_call(functools.partial(scatter_kernel, planes, count), out_shap...  153 us
    dot_general x1, matrix products, on_device(): jnp.einsum('tf,df->td', inner, up, preferred_element_type=jnp.float32)  16.3 us
    dot_general x1, matrix products, on_device(): jnp.einsum('td,fd->tf', rows_g, down, preferred_element_type=jnp.float32)  15.6 us
    dot_general x1, matrix products, on_device(): out = jnp.dot(active, down, preferred_element_type=jnp.float32)  12.8 us
    dot_general x1, matrix products, on_device(): pre = jnp.dot(rows_a, up, preferred_element_type=jnp.float32)  12.7 us
    dot_general x1, matrix products, on_device(): pre = jnp.dot(rows_b, up, preferred_element_type=jnp.float32)  11.3 us
  transfers between devices with their start and end apart: 1, of which 0 were waited for; matrix products, arithmetic and copies ran while one was open for 10% of the time, Pallas kernels for 33%

profile of v3, /device:TPU:0, one launch (start us, length us, event | category | flops | bytes accessed | tf_op | source)
XLA Modules:
  0.0 458.1 jit_solution(265663370917610062)
XLA Ops:
  0.6 1.2 multiply_reduce_fusion.1
  1.9 1.2 fusion.22
  3.1 0.1 rsqrt.30
  3.2 0.1 rsqrt.28
  3.3 0.7 fusion.40
  4.0 0.7 fusion.41
  4.7 1.3 fusion.18
  6.1 1.3 fusion.14
  7.4 0.1 copy.42
  7.5 0.6 pad.8.clone
  8.1 2.3 multiply_convert_fusion.6
  10.4 193.3 %shard_map.103 = (bf16[16,2,32,3584]{3,2,1,0:T(8,128)(2,1)}, bf16[16,2,32,3584]{3,2,1,0:T(8,128)(2,1)}, bf16[16,2,32,3584]{3,2,1,0:T(8,128)(2,1)}, f32[16,2,32,128]{3,2,1,0:T(8,128)}) custom-call(bf16[2,32,3584]{2,1,0:T(8,128)(2,1)} %get-tuple-element.28.refs_0_, bf16[2,32,3584]{2,1,0:T(8,128)(2,1)} %get-tuple-element.27.refs_1_, ...), custom_call_target="tpu_custom_call" | custom-call | tf_op jit(solution)/shard_map/pallas_call | solution.py:155
  203.7 1.7 slice_reduce_fusion
  205.4 0.2 copy.41
  205.6 11.3 %fusion.4 = f32[1024,1024]{1,0:T(8,128)S(1)} fusion(bf16[1024,3584]{1,0:T(8,128)(2,1)} %bitcast.97, bf16[1,1,3584,1024]{3,2,1,0:T(8,128)(2,1)} %param.14), kind=kOutput, calls=%fused_computation.6 | convolution fusion | flops 7516192768 | bytes 18874368 | tf_op jit(solution)/shard_map/dot_general | solution.py:383
  216.9 15.6 %multiply_reduce_fusion = (f32[1024]{0:T(1024)S(1)}, f32[1024,1024]{1,0:T(8,128)}) fusion(f32[1024,1024]{1,0:T(8,128)S(1)} %fusion.4, bf16[1024,3584]{1,0:T(8,128)(2,1)} %bitcast.116, bf16[1,1,1024,3584]{3,2,1,0:T(8,128)(2,1)} %param.15), kind=kOutput, calls=%fused_computation.11 | convolution fusion | flops 7522483200 | bytes 23072768 | tf_op jit(solution)/shard_map/td,fd->tf/dot_general | solution.py:384
  232.5 0.6 pad_bitcast_fusion.refs_0_
  233.1 17.8 %shard_map.105 = f32[16,2,8,128]{3,2,1,0:T(8,128)} custom-call(f32[2,8,128]{2,1,0:T(8,128)} %pad_bitcast_fusion.refs_0_), custom_call_target="tpu_custom_call" | custom-call | tf_op jit(solution)/shard_map/pallas_call | solution.py:155
  250.9 0.9 copy.48
  251.9 5.1 %fusion.43 = f32[1,3584]{1,0:T(1,128)S(1)} fusion(bf16[1024,3584]{1,0:T(8,128)(2,1)} %bitcast.98, f32[1024,16]{0,1:T(8,128)S(1)} %get-tuple-element.19, s32[]{:T(128)S(6)} %select_n.21), kind=kOutput, calls=%fused_computation.70 | convolution fusion | flops 44040192 | bytes 7358468 | tf_op jit(solution)/shard_map/dot_general | solution.py:407
  257.0 12.7 %multiply_convert_fusion.3 = bf16[1024,1024]{1,0:T(8,128)(2,1)S(1)} fusion(bf16[1024,3584]{1,0:T(8,128)(2,1)} %bitcast.115, bf16[1,1,3584,1024]{3,2,1,0:T(8,128)(2,1)} %param.14), kind=kOutput, calls=%fused_computation.14 | convolution fusion | flops 7521435648 | bytes 16777216 | tf_op jit(solution)/shard_map/dot_general | solution.py:377
  269.8 0.2 constant_dynamic-slice_fusion.1
  270.0 0.2 copy.45
  270.2 16.3 %multiply_convert_fusion = bf16[1024,3584]{1,0:T(8,128)(2,1)} fusion(bf16[1,1,3584,1024]{3,2,1,0:T(8,128)(2,1)} %param.14, f32[1024]{0:T(1024)S(1)} %bitcast.114, f32[1024,1024]{1,0:T(8,128)} %get-tuple-element.24, f32[1024,1024]{1,0:T(8,128)} %copy-done.4), kind=kOutput, calls=%fused_computation | convolution fusion | flops 7532969984 | bytes 23072768 | tf_op jit(solution)/shard_map/tf,df->td/dot_general | solution.py:388
  286.6 12.8 %multiply_convert_fusion.1 = bf16[1024,3584]{1,0:T(8,128)(2,1)} fusion(bf16[1024,1024]{1,0:T(8,128)(2,1)S(1)} %multiply_convert_fusion.3, bf16[1,1,1024,3584]{3,2,1,0:T(8,128)(2,1)} %param.15, f32[1024]{0:T(1024)S(1)} %bitcast.111), kind=kOutput, calls=%fused_computation.1 | convolution fusion | flops 7523532800 | bytes 16781312 | tf_op jit(solution)/shard_map/dot_general | solution.py:379
  299.4 153.1 %shard_map.104 = (bf16[2,32,3584]{2,1,0:T(8,128)(2,1)}, bf16[2,32,3584]{2,1,0:T(8,128)(2,1)}) custom-call(bf16[16,2,32,3584]{3,2,1,0:T(8,128)(2,1)} %bitcast.100, bf16[16,2,32,3584]{3,2,1,0:T(8,128)(2,1)} %bitcast.99), custom_call_target="tpu_custom_call" | custom-call | tf_op jit(solution)/shard_map/pallas_call | solution.py:311
  452.5 1.1 convert_multiply_fusion.2
  453.6 1.1 convert_multiply_fusion.1
  454.7 0.8 fusion.24
  455.6 1.1 fusion.30
  456.6 0.8 fusion.21
  457.5 0.6 add_bitcast_fusion
  (20 shorter events, 0.2 us)
Async XLA Ops:
  0.6 4.1 copy-start
  216.9 15.6 %copy-start.4 = (f32[1024,1024]{1,0:T(8,128)}, f32[1024,1024]{1,0:T(8,128)S(1)}, u32[]{:S(2)}) copy-start(f32[1024,1024]{1,0:T(8,128)S(1)} %fusion.4) | copy-start | bytes 12582916
  257.0 200.5 %collective-permute-start = (f32[1,3584]{1,0:T(1,128)S(1)}, f32[1,3584]{1,0:T(1,128)S(1)}, u32[]{:S(2)}, u32[]{:S(2)}) collective-permute-start(f32[1,3584]{1,0:T(1,128)S(1)} %fusion.43), channel_id=1, source_target_pairs={{0,16},{16,0},{1,17},{17,1},{2,18},{18,2},{3,19},{19,3},{4,20},{20... | collective-permute-start | bytes 43016 | tf_op jit(solution)/shard_map/ppermute | solution.py:21
  299.4 155.3 %copy-start.1 = (bf16[1,64,3584]{2,1,0:T(8,128)(2,1)S(1)}, bf16[1,64,3584]{2,1,0:T(8,128)(2,1)}, u32[]{:S(2)}) copy-start(bf16[1,64,3584]{2,1,0:T(8,128)(2,1)} %param.10) | copy-start | bytes 1376260
  299.4 156.2 %copy-start.3 = (bf16[1,64,3584]{2,1,0:T(8,128)(2,1)S(1)}, bf16[1,64,3584]{2,1,0:T(8,128)(2,1)}, u32[]{:S(2)}) copy-start(bf16[1,64,3584]{2,1,0:T(8,128)(2,1)} %param.12) | copy-start | bytes 1376260
  452.5 4.2 copy-start.2
